TPU v7x, 512 devices: a whole 4x8x8 slice. The times are simulated.
512 devices in a mesh: row: 32 (over x, y), col: 16 (over z, core).
Axes of the slice: x: 4, y: 8, z: 8, core: 2. Of those that a mesh axis runs over, the one named last changes fastest.
Arguments:
- amplitudes: bfloat16 [32768, 32768], P('row', 'col'), may hold values from -6 to 6
- integrals: bfloat16 [32768, 1024], P('col', 'row'), may hold values from -0.03125 to 0.03125
- tile_mask: int32 [256, 256], P('row', 'col'), may hold values 0 or 1
Outputs:
- residual: bfloat16 [32768, 1024], P('row', 'col')
All inputs are finite; a program needn't handle non-finite values. No bound on the sum of `tile_mask` on one device may be relied on, other than what follows from the above.
Results may differ from a plain program's by a relative error of at most 0.001.
Values may be sent and summed in bfloat16 or wider, within the bound.
A program may use at most 64 MiB of HBM per device.

v0:
```python
import jax
import jax.numpy as jnp
from jax import lax
from jax.sharding import PartitionSpec as P


def apply_mask(amplitudes, tile_mask):
    tiles_m, tiles_k = tile_mask.shape
    tile_rows = amplitudes.shape[0] // tiles_m
    tile_cols = amplitudes.shape[1] // tiles_k
    blocks = amplitudes.reshape(tiles_m, tile_rows, tiles_k, tile_cols)
    weights = tile_mask.astype(amplitudes.dtype)[:, None, :, None]
    return (blocks * weights).reshape(amplitudes.shape)


def per_device(amplitudes, integrals, tile_mask):
    masked = apply_mask(amplitudes, tile_mask)
    partial_sums = jnp.dot(
        masked,
        lax.all_gather(integrals, "row", axis=1, tiled=True),
        preferred_element_type=jnp.float32,
    )
    summed = lax.psum_scatter(partial_sums, "col", scatter_dimension=1, tiled=True)
    return summed.astype(jnp.bfloat16)


def solution(mesh):
    placed = (P("row", "col"), P("col", "row"), P("row", "col"))
    return jax.shard_map(
        per_device, mesh=mesh, in_specs=placed, out_specs=P("row", "col"), check_vma=False
    )
```

profile of v0, /device:TPU:1, one launch (start us, length us, event | category | flops | bytes accessed | tf_op | source)
XLA Modules:
  0.0 183.2 jit_solution(4674022924054727534)
XLA Ops:
  6.5 0.0 all-gather.2.cloned.1.call-start
  6.5 0.7 all-gather.2.cloned.1.call-update
  7.3 0.0 reduce-scatter.2.cloned.1.call-start
  7.3 0.7 convert_element_type.6
  8.0 92.4 %all-gather.2.cloned.1.call-done = bf16[2048,1024]{0,1:T(8,128)(2,1)} async-done(((bf16[2048,32]{0,1:T(8,128)(2,1)}), bf16[2048,1024]{0,1:T(8,128)(2,1)}) %all-gather.2.cloned.1.call-update) | async-done | bytes 4194320 | tf_op jit(solution)/shard_map/all_gather | solution.py:20
  100.4 0.0 copy-start
  100.4 0.6 mul.11
  101.1 1.6 copy-done
  102.6 8.5 %fusion = f32[1024,1024]{0,1:T(8,128)} fusion(bf16[2048,1024]{0,1:T(8,128)(2,1)} %all-gather.2.cloned.1.call-done, bf16[1024,2048]{1,0:T(8,128)(2,1)S(1)} %copy-done, bf16[128,8,16,128]{3,2,1,0:T(8,128)(2,1)S(1)} %bitcast.6), kind=kOutput, calls=%fused_computation.1 | convolution fusion | flops 4297064448 | bytes 16777216 | tf_op jit(solution)/shard_map/dot_general | solution.py:18
  111.2 0.0 reduce-scatter.2.cloned.1.call-update
  111.2 63.5 %reduce-scatter.2.cloned.1.call-done = f32[1024,64]{0,1:T(8,128)} async-done(((f32[1024,1024]{0,1:T(8,128)}), f32[1024,64]{0,1:T(8,128)}) %reduce-scatter.2.cloned.1.call-update) | async-done | bytes 262160 | tf_op jit(solution)/shard_map/reduce_scatter | solution.py:23
  174.7 1.6 convert_element_type.7
Async XLA Ops:
  6.5 93.9 %all-gather.2.cloned.1.call-start = ((), (), s32[]{:S(2)}) async-start(), calls=%async_computation.1 | async-start | bytes 4325376 | tf_op jit(solution)/shard_map/all_gather | solution.py:20
  7.3 167.5 %reduce-scatter.2.cloned.1.call-start = ((), (), s32[]{:S(2)}) async-start(), calls=%async_computation.2 | async-start | bytes 4456448 | tf_op jit(solution)/shard_map/reduce_scatter | solution.py:23
  100.4 2.2 %copy-start = (bf16[1024,2048]{1,0:T(8,128)(2,1)S(1)}, bf16[1024,2048]{1,0:T(8,128)(2,1)}, u32[]{:S(2)}) copy-start(bf16[1024,2048]{1,0:T(8,128)(2,1)} %param.3) | copy-start | bytes 12582916
Sparse Core Ops, SparseCore 0:
  10.5 89.8 all-gather.1
  111.3 63.3 reduce-scatter.1
where the time goes:
time: 186 us; the launch traced here: 183 us
  waiting for transfers between devices  157 us (84%)
  between operations  13.4 us (7%)
  matrix products  8.55 us (5%)
  other arithmetic  2.31 us (1%)
  local copies, waits for them, and re-layouts  2.18 us (1%)
    all_gather x1, waiting for transfers between devices, per_device(): lax.all_gather(integrals, 'row', axis=1, tiled=True)  92.4 us
    reduce_scatter x1, waiting for transfers between devices, per_device(): lax.psum_scatter(partial_sums, 'col', scatter_dimension=1, tiled=True)  63.5 us
    dot_general x1, matrix products, per_device(): jnp.dot(masked, lax.all_gather(integrals, 'row', axis=1, tiled=True), pre...  8.55 us
  transfers between devices with their start and end apart: 2, of which 2 were waited for; matrix products, arithmetic and copies ran while one was open for 0% of the time, Pallas kernels for 0%

commit v1 on v0

v1 whole, which is shorter than its diff:
```python
import jax
import jax.numpy as jnp
from jax import lax
from jax.experimental import pallas as pl
from jax.experimental.pallas import tpu as pltpu
from jax.sharding import PartitionSpec as P

MESH = pl.DeviceIdType.MESH
NX, NY, NZ = 4, 8, 8
TILE = 128
SHARD = 32
ROWS = 1024
DEPTH = 2048
HALF = ROWS // 2
BLOCK = 256
SPLIT = 768

FIRST = slice(0, SPLIT)
REST = slice(SPLIT, DEPTH)
FIRST_A = slice(0, SPLIT // 2)
FIRST_B = slice(SPLIT // 2, SPLIT)
REST_A = slice(SPLIT, (SPLIT + DEPTH) // 2)
REST_B = slice((SPLIT + DEPTH) // 2, DEPTH)
N_SEND = 120


def shard(j):
    return slice(j * SHARD, (j + 1) * SHARD)


def kernel(a_hbm, own, mask, out, a, bt, cb, xb, rb, fin, done, lsem, ssem, ag, ex, ch, fs):
    row, col = lax.axis_index("row"), lax.axis_index("col")
    x, y = row // NY, row % NY
    z, core = col // 2, col % 2
    xp = (((x + 1) % NX) * NY + y, col)
    xm = (((x + NX - 1) % NX) * NY + y, col)
    yp = (x * NY + (y + 1) % NY, col)
    ym = (x * NY + (y + NY - 1) % NY, col)
    sigma = 1 - 2 * core
    ahead = (row, ((z + NZ + sigma) % NZ) * 2 + core)
    behind = (row, ((z + NZ - sigma) % NZ) * 2 + core)
    partner = (row, z * 2 + 1 - core)

    load_a = pltpu.make_async_copy(a_hbm, a, lsem.at[0])
    load_b = pltpu.make_async_copy(own, bt.at[0, shard(0)], lsem.at[1])
    load_a.start()
    load_b.start()

    barrier = pltpu.get_barrier_semaphore()
    for dev in (xp, xm, yp, ym, ahead, behind, partner):
        pl.semaphore_signal(barrier, inc=1, device_id=dev, device_id_type=MESH)
    pl.semaphore_wait(barrier, 7)

    pending = []
    count = [0]

    def copy_of(src, dst, send_sem, recv_sem, dev):
        return pltpu.make_async_remote_copy(
            src_ref=src, dst_ref=dst, send_sem=send_sem, recv_sem=recv_sem, device_id=dev, device_id_type=MESH
        )

    def send(src, dst, recv_sem, dev):
        copy = copy_of(src, dst, ssem.at[count[0]], recv_sem, dev)
        count[0] += 1
        copy.start()
        pending.append((None, copy))

    def arrive(dst, recv_sem):
        copy_of(dst, dst, ssem.at[0], recv_sem, partner).wait_recv()

    def origin(q):
        step = (q + 1) // 2
        return (y + NY - step) % NY if q % 2 == 1 else (y + step) % NY

    def own_sends():
        for dev, j, k in ((xp, 3, 2), (xm, 1, 3)):
            send(own.at[:, FIRST], bt.at[0, shard(j), FIRST], ag.at[0, k], dev)
        for dev, q in ((yp, 1), (ym, 2)):
            send(own.at[:, REST], bt.at[q, shard(0), REST], ag.at[q, 0], dev)
            send(own.at[:, FIRST], bt.at[q, shard(0), FIRST], ag.at[q, 2], dev)
        for dev, j, k in ((xp, 3, 6), (xm, 1, 7)):
            send(own.at[:, REST], bt.at[0, shard(j), REST], ag.at[0, k], dev)

    def own_gather():
        arrive(bt.at[0, shard(3), FIRST], ag.at[0, 2])
        send(bt.at[0, shard(3), FIRST_A], bt.at[0, shard(2), FIRST_A], ag.at[0, 4], xp)
        for dev, q in ((yp, 1), (ym, 2)):
            send(bt.at[0, shard(3), FIRST], bt.at[q, shard(3), FIRST], ag.at[q, 5], dev)
        arrive(bt.at[0, shard(1), FIRST], ag.at[0, 3])
        send(bt.at[0, shard(1), FIRST_B], bt.at[0, shard(2), FIRST_B], ag.at[0, 5], xm)
        for dev, q in ((yp, 1), (ym, 2)):
            send(bt.at[0, shard(1), FIRST], bt.at[q, shard(1), FIRST], ag.at[q, 3], dev)

    def own_gather_far():
        arrive(bt.at[0, shard(2), FIRST_A], ag.at[0, 4])
        arrive(bt.at[0, shard(2), FIRST_B], ag.at[0, 5])
        for dev, q in ((yp, 1), (ym, 2)):
            send(bt.at[0, shard(2), FIRST], bt.at[q, shard(2), FIRST], ag.at[q, 4], dev)

    def across(q):
        send(bt.at[q, shard(0), REST], bt.at[q, shard(3), REST], ag.at[q, 6], xp)
        send(bt.at[q, shard(0), REST], bt.at[q, shard(1), REST], ag.at[q, 7], xm)

    def take_rest(q):
        if q == 7:
            arrive(bt.at[7, shard(0), REST_A], ag.at[7, 0])
            arrive(bt.at[7, shard(0), REST_B], ag.at[7, 1])
            across(7)
            return
        dev = yp if q % 2 == 1 else ym
        arrive(bt.at[q, shard(0), REST], ag.at[q, 0])
        if q < 5:
            send(bt.at[q, shard(0), REST], bt.at[q + 2, shard(0), REST], ag.at[q + 2, 0], dev)
        elif q == 5:
            send(bt.at[5, shard(0), REST_A], bt.at[7, shard(0), REST_A], ag.at[7, 0], dev)
        else:
            send(bt.at[6, shard(0), REST_B], bt.at[7, shard(0), REST_B], ag.at[7, 1], dev)
        across(q)

    def take_first(q, j):
        dev = yp if q % 2 == 1 else ym
        arrive(bt.at[q, shard(j), FIRST], ag.at[q, 2 + j])
        if q < 5:
            send(bt.at[q, shard(j), FIRST], bt.at[q + 2, shard(j), FIRST], ag.at[q + 2, 2 + j], dev)
        elif (q == 5 and j in (0, 3)) or (q == 6 and j in (1, 2)):
            send(bt.at[q, shard(j), FIRST], bt.at[7, shard(j), FIRST], ag.at[7, 2 + j], dev)

    def relay(q):
        arrive(bt.at[q, shard(3), REST], ag.at[q, 6])
        send(bt.at[q, shard(3), REST_A], bt.at[q, shard(2), REST_A], ag.at[q, 8], xp)
        arrive(bt.at[q, shard(1), REST], ag.at[q, 7])
        send(bt.at[q, shard(1), REST_B], bt.at[q, shard(2), REST_B], ag.at[q, 9], xm)

    def take_far(q):
        arrive(bt.at[q, shard(2), REST_A], ag.at[q, 8])
        arrive(bt.at[q, shard(2), REST_B], ag.at[q, 9])

    def multiply(q, which, i):
        start = pl.multiple_of(which * HALF + i * BLOCK, BLOCK)
        cb[q, which, :, i * BLOCK : (i + 1) * BLOCK] = lax.dot_general(
            bt[q], a[pl.ds(start, BLOCK), :], (((1,), (1,)), ((), ())), preferred_element_type=jnp.float32
        )

    def swap(q):
        send(cb.at[q, 1 - core], xb.at[q], ex.at[q], partner)

    def spot(q, delta):
        h = origin(q) // 4
        e = (z + NZ - h) % NZ
        j = ((e + delta + NZ) // 2 + NX - x) % NX
        return cb.at[q, core, pl.ds(pl.multiple_of(j * SHARD, SHARD), SHARD), :]

    def is_even(q):
        return (z + origin(q) // 4) % 2 == 0

    base = 84

    def pass_on(q, cond, src, slot, sem, dev):
        copy = copy_of(src, rb.at[q, slot], ssem.at[base + 4 * q + sem], ch.at[q, slot], dev)
        copy.start()
        pending.append((cond, copy))

    def merge(q):
        arrive(xb.at[q], ex.at[q])
        cb[q, core] += xb[q]

    def stage1(q):
        even = is_even(q)

        @pl.when(even)
        def _():
            pass_on(q, "even", spot(q, 4), 0, 0, ahead)

    def stage2(q):
        even = is_even(q)

        @pl.when(jnp.logical_not(even))
        def _():
            pass_on(q, "odd", spot(q, -3 * sigma), 1, 1, behind)
            arrive(rb.at[q, 0], ch.at[q, 0])
            here = spot(q, 3 * sigma)
            here[...] += rb[q, 0]
            pass_on(q, "odd", here, 0, 0, ahead)

    def stage3(q):
        even = is_even(q)

        @pl.when(even)
        def _():
            for slot, sign, dev in ((1, -1, behind), (0, 1, ahead)):
                arrive(rb.at[q, slot], ch.at[q, slot])
                here = spot(q, 2 * sign * sigma)
                here[...] += rb[q, slot]
                pass_on(q, "even", here, 2 + slot, 1 + slot, dev)

    def stage4(q):
        even = is_even(q)

        @pl.when(jnp.logical_not(even))
        def _():
            for slot, sign, dev in ((1, -1, behind), (0, 1, ahead)):
                arrive(rb.at[q, 2 + slot], ch.at[q, 2 + slot])
                here = spot(q, sign * sigma)
                here[...] += rb[q, 2 + slot]
                pass_on(q, "odd", here, 2 + slot, 2 + slot, dev)

    def place(ref, index):
        columns = pl.ds(pl.multiple_of(core * HALF, HALF), HALF)
        return ref.at[index, :, columns]

    def finish(q):
        even = is_even(q)
        origin_y = origin(q)
        index = origin_y % 2
        mine = (origin_y // 2) % 2 == core

        @pl.when(even)
        def _():
            arrive(rb.at[q, 2], ch.at[q, 2])
            arrive(rb.at[q, 3], ch.at[q, 3])
            total = (spot(q, 0)[...] + rb[q, 2] + rb[q, 3]).astype(jnp.bfloat16)

            @pl.when(mine)
            def _():
                place(done, index)[...] = total

            @pl.when(jnp.logical_not(mine))
            def _():
                fin[index] = total
                copy_of(fin.at[index], place(done, index), fs.at[0, index], fs.at[1, index], partner).start()

    own_sends()
    own_gather()
    load_a.wait()

    def apply_mask(i, carry):
        rows = pl.ds(pl.multiple_of(i * TILE, TILE), TILE)
        for k in range(DEPTH // TILE):
            cols = slice(k * TILE, (k + 1) * TILE)
            a[rows, cols] = jnp.where(mask[i, k] != 0, a[rows, cols], jnp.zeros((TILE, TILE), jnp.bfloat16))
        return carry

    lax.fori_loop(0, ROWS // TILE, apply_mask, 0)
    own_gather_far()
    load_b.wait()

    for t in range(1, 15):
        for q, step in ((t - 7, finish), (t - 6, stage4), (t - 5, stage3), (t - 4, stage2)):
            if 0 <= q < 8:
                step(q)
        if 0 <= t - 3 < 8:
            merge(t - 3)
            stage1(t - 3)
        if 0 <= t - 1 < 8:
            relay(t - 1)
        work = []
        if 0 <= t - 2 < 8:
            q = t - 2
            take_far(q)
            work = [(q, 1 - core, 0), (q, 1 - core, 1), (q, core, 0), (q, core, 1)]
        takes = []
        if t < 8:
            takes = [None] + [0, 3, 1, 2]
        for i in range(5):
            if i < len(takes):
                if takes[i] is None:
                    take_rest(t)
                else:
                    take_first(t, takes[i])
            if i < len(work):
                multiply(*work[i])
                if i == 1:
                    swap(t - 2)

    for index in range(2):
        @pl.when(True)
        def _():
            half = pl.ds(pl.multiple_of((1 - core) * HALF, HALF), HALF)
            arrive(done.at[index, :, half], fs.at[1, index])
            copy_of(fin.at[index], place(done, index), fs.at[0, index], fs.at[1, index], partner).wait_send()
    for index in range(2):
        out[index * SHARD : (index + 1) * SHARD, :] = done[index]

    for cond, copy in pending:
        if cond is None:
            copy.wait_send()
    for q in range(8):
        even = is_even(q)
        parts = {"even": [c for p, c in pending if p == "even"], "odd": [c for p, c in pending if p == "odd"]}
        del parts

        @pl.when(even)
        def _():
            for slot in range(3):
                copy_of(rb.at[q, 0], rb.at[q, 0], ssem.at[base + 4 * q + slot], ch.at[q, 0], partner).wait_send()

        @pl.when(jnp.logical_not(even))
        def _():
            for slot in range(4):
                copy_of(rb.at[q, 0], rb.at[q, 0], ssem.at[base + 4 * q + slot], ch.at[q, 0], partner).wait_send()


def per_device(amplitudes, integrals, tile_mask):
    result = pl.pallas_call(
        kernel,
        out_shape=jax.ShapeDtypeStruct((2 * SHARD, ROWS), jnp.bfloat16),
        in_specs=[
            pl.BlockSpec(memory_space=pl.ANY),
            pl.BlockSpec(memory_space=pl.ANY),
            pl.BlockSpec(memory_space=pltpu.SMEM),
        ],
        out_specs=pl.BlockSpec(memory_space=pltpu.VMEM),
        scratch_shapes=[
            pltpu.VMEM((ROWS, DEPTH), jnp.bfloat16),
            pltpu.VMEM((8, 4 * SHARD, DEPTH), jnp.bfloat16),
            pltpu.VMEM((8, 2, 4 * SHARD, HALF), jnp.float32),
            pltpu.VMEM((8, 4 * SHARD, HALF), jnp.float32),
            pltpu.VMEM((8, 4, SHARD, HALF), jnp.float32),
            pltpu.VMEM((2, SHARD, HALF), jnp.bfloat16),
            pltpu.VMEM((2, SHARD, ROWS), jnp.bfloat16),
            pltpu.SemaphoreType.DMA((2,)),
            pltpu.SemaphoreType.DMA((N_SEND,)),
            pltpu.SemaphoreType.DMA((8, 10)),
            pltpu.SemaphoreType.DMA((8,)),
            pltpu.SemaphoreType.DMA((8, 4)),
            pltpu.SemaphoreType.DMA((2, 2)),
        ],
        compiler_params=pltpu.CompilerParams(
            collective_id=0, has_side_effects=True, vmem_limit_bytes=60 * 1024 * 1024
        ),
    )(amplitudes, integrals.T, tile_mask)
    return result.T


def solution(mesh):
    placed = (P("row", "col"), P("col", "row"), P("row", "col"))
    return jax.shard_map(
        per_device, mesh=mesh, in_specs=placed, out_specs=P("row", "col"), check_vma=False
    )
```

time: 186 us -> 83.1 us (0.45)
  waiting for transfers between devices: 157 us -> 0 us
  Pallas kernels: 0 us -> 80.3 us
  between operations: 13.4 us -> 0.01 us
  matrix products: 8.55 us -> 0 us
  other arithmetic: 2.31 us -> 0 us
    all_gather x1 -> x0, waiting for transfers between devices: 92.4 us -> none  [per_device(): lax.all_gather(integrals, 'row', axis=1, tiled=True)]
    pallas_call x0 -> x1, Pallas kernels: none -> 80.3 us  [per_device(): pl.pallas_call(kernel, out_shape=jax.ShapeDtypeStruct((2 * SHARD, ROWS),...]
    reduce_scatter x1 -> x0, waiting for transfers between devices: 63.5 us -> none  [per_device(): lax.psum_scatter(partial_sums, 'col', scatter_dimension=1, tiled=True)]
    dot_general x1 -> x0, matrix products: 8.55 us -> none  [per_device(): jnp.dot(masked, lax.all_gather(integrals, 'row', axis=1, tiled=True), pre...]
    convert_element_type x2 -> x0, other arithmetic: 2.31 us -> none  [the longest x1 1.62 us: per_device(): return summed.astype(jnp.bfloat16)]
  transfers between devices with their start and end apart: 2 -> 0, of which waited for: 2 -> 0; matrix products, arithmetic and copies ran while one was open for 0% -> 0% of each run, Pallas kernels for 0% -> 0%
where the time goes in v1:
time: 83.1 us; the launch traced here: 81.9 us
  Pallas kernels  80.3 us (97%)
  local copies, waits for them, and re-layouts  1.57 us (2%)
    pallas_call x1, Pallas kernels, per_device(): pl.pallas_call(kernel, out_shape=jax.ShapeDtypeStruct((2 * SHARD, ROWS),...  80.3 us

profile of v1, /device:TPU:1, one launch (start us, length us, event | category | flops | bytes accessed | tf_op | source)
XLA Modules:
  0.0 81.9 jit_solution(1882440143425356045)
XLA Ops:
  0.0 80.3 %shard_map.37 = bf16[64,1024]{1,0:T(8,128)(2,1)} custom-call(bf16[1024,2048]{1,0:T(8,128)(2,1)} %a_hbm.1, bf16[32,2048]{1,0:T(8,128)(2,1)} %bitcast.3, s32[8,16]{1,0:T(8,128)} %mask.1), custom_call_target="tpu_custom_call" | custom-call | tf_op jit(solution)/shard_map/pallas_call | solution.py:304
  80.3 1.6 %copy.5 = bf16[1024,64]{0,1:T(8,128)(2,1)} copy(bf16[1024,64]{0,1:T(8,128)(2,1)} %bitcast.2) | data formatting | bytes 262144

commit v2 on v1

v2 whole, which is shorter than its diff:
```python
import jax
import jax.numpy as jnp
from jax import lax
from jax.experimental import pallas as pl
from jax.experimental.pallas import tpu as pltpu
from jax.sharding import PartitionSpec as P

MESH = pl.DeviceIdType.MESH
NX, NY, NZ = 4, 8, 8
TILE = 128
SHARD = 32
ROWS = 1024
DEPTH = 2048
HALF = ROWS // 2
BLOCK = 256
SPLIT = 768

FIRST = slice(0, SPLIT)
REST = slice(SPLIT, DEPTH)
FIRST_A = slice(0, SPLIT // 2)
FIRST_B = slice(SPLIT // 2, SPLIT)
REST_A = slice(SPLIT, (SPLIT + DEPTH) // 2)
REST_B = slice((SPLIT + DEPTH) // 2, DEPTH)
BASE = 100
N_SEND = BASE + 32
FAST = (7,)


def shard(j):
    return slice(j * SHARD, (j + 1) * SHARD)


def kernel(a_hbm, own, mask, out, a, bt, cb, xb, rb, fb, fin, done, lsem, ssem, ag, ex, ch, fch, fs):
    row, col = lax.axis_index("row"), lax.axis_index("col")
    x, y = row // NY, row % NY
    z, core = col // 2, col % 2
    xp = (((x + 1) % NX) * NY + y, col)
    xm = (((x + NX - 1) % NX) * NY + y, col)
    yp = (x * NY + (y + 1) % NY, col)
    ym = (x * NY + (y + NY - 1) % NY, col)
    sigma = 1 - 2 * core
    ahead = (row, ((z + NZ + sigma) % NZ) * 2 + core)
    behind = (row, ((z + NZ - sigma) % NZ) * 2 + core)
    partner = (row, z * 2 + 1 - core)

    def along_z(delta):
        return (row, ((z + NZ + delta) % NZ) * 2 + core)


    load_a = pltpu.make_async_copy(a_hbm, a, lsem.at[0])
    load_b = pltpu.make_async_copy(own, bt.at[0, shard(0)], lsem.at[1])
    load_a.start()
    load_b.start()

    barrier = pltpu.get_barrier_semaphore()
    for dev in [xp, xm, yp, ym, partner] + [along_z(d) for d in (1, -1, 2, -2, 3, -3)]:
        pl.semaphore_signal(barrier, inc=1, device_id=dev, device_id_type=MESH)
    pl.semaphore_wait(barrier, 11)

    pending = []
    count = [0]

    def copy_of(src, dst, send_sem, recv_sem, dev):
        return pltpu.make_async_remote_copy(
            src_ref=src, dst_ref=dst, send_sem=send_sem, recv_sem=recv_sem, device_id=dev, device_id_type=MESH
        )

    def send(src, dst, recv_sem, dev):
        copy = copy_of(src, dst, ssem.at[count[0]], recv_sem, dev)
        count[0] += 1
        copy.start()
        pending.append(copy)

    def arrive(dst, recv_sem):
        copy_of(dst, dst, ssem.at[0], recv_sem, partner).wait_recv()

    def origin(q):
        step = (q + 1) // 2
        return (y + NY - step) % NY if q % 2 == 1 else (y + step) % NY

    def own_first_x():
        for dev, j, k in ((xp, 3, 2), (xm, 1, 3)):
            send(own.at[:, FIRST], bt.at[0, shard(j), FIRST], ag.at[0, k], dev)

    def own_rest_y():
        for dev, q in ((yp, 1), (ym, 2)):
            send(own.at[:, REST], bt.at[q, shard(0), REST], ag.at[q, 0], dev)

    def own_first_y():
        for dev, q in ((yp, 1), (ym, 2)):
            send(own.at[:, FIRST], bt.at[q, shard(0), FIRST], ag.at[q, 2], dev)

    def across_a(q, src):
        send(src.at[:, REST_A], bt.at[q, shard(3), REST_A], ag.at[q, 6], xp)
        send(src.at[:, REST_A], bt.at[q, shard(1), REST_A], ag.at[q, 10], xm)

    def across_b(q, src):
        send(src.at[:, REST_B], bt.at[q, shard(1), REST_B], ag.at[q, 7], xm)
        send(src.at[:, REST_B], bt.at[q, shard(3), REST_B], ag.at[q, 11], xp)

    def across(q, src):
        send(src.at[:, REST_A], bt.at[q, shard(3), REST_A], ag.at[q, 6], xp)
        send(src.at[:, REST_B], bt.at[q, shard(1), REST_B], ag.at[q, 7], xm)
        send(src.at[:, REST_B], bt.at[q, shard(3), REST_B], ag.at[q, 11], xp)
        send(src.at[:, REST_A], bt.at[q, shard(1), REST_A], ag.at[q, 10], xm)

    def own_rest_x():
        across(0, own)

    def gather(j):
        dev, half, k = (xp, FIRST_A, 4) if j == 3 else (xm, FIRST_B, 5)
        arrive(bt.at[0, shard(j), FIRST], ag.at[0, 2 if j == 3 else 3])
        send(bt.at[0, shard(j), half], bt.at[0, shard(2), half], ag.at[0, k], dev)
        for dev, q in ((yp, 1), (ym, 2)):
            send(bt.at[0, shard(j), FIRST], bt.at[q, shard(j), FIRST], ag.at[q, 2 + j], dev)

    def gather_far():
        arrive(bt.at[0, shard(2), FIRST_A], ag.at[0, 4])
        arrive(bt.at[0, shard(2), FIRST_B], ag.at[0, 5])
        for dev, q in ((yp, 1), (ym, 2)):
            send(bt.at[0, shard(2), FIRST], bt.at[q, shard(2), FIRST], ag.at[q, 4], dev)

    def take_rest(q):
        dev = yp if q % 2 == 1 else ym
        arrive(bt.at[q, shard(0), REST], ag.at[q, 0])
        if q < 5:
            send(bt.at[q, shard(0), REST], bt.at[q + 2, shard(0), REST], ag.at[q + 2, 0], dev)
        elif q == 5:
            send(bt.at[5, shard(0), REST_A], bt.at[7, shard(0), REST_A], ag.at[7, 0], dev)
        else:
            send(bt.at[6, shard(0), REST_B], bt.at[7, shard(0), REST_B], ag.at[7, 1], dev)
        across(q, bt.at[q, shard(0)])

    def take_rest_far(source):
        if source == 5:
            arrive(bt.at[7, shard(0), REST_A], ag.at[7, 0])
            across_a(7, bt.at[7, shard(0)])
        else:
            arrive(bt.at[7, shard(0), REST_B], ag.at[7, 1])
            across_b(7, bt.at[7, shard(0)])

    def take_first(q, j):
        dev = yp if q % 2 == 1 else ym
        arrive(bt.at[q, shard(j), FIRST], ag.at[q, 2 + j])
        if q < 5:
            send(bt.at[q, shard(j), FIRST], bt.at[q + 2, shard(j), FIRST], ag.at[q + 2, 2 + j], dev)
        elif (q == 5 and j in (0, 3)) or (q == 6 and j in (1, 2)):
            send(bt.at[q, shard(j), FIRST], bt.at[7, shard(j), FIRST], ag.at[7, 2 + j], dev)

    def relay(q, j):
        if j == 3:
            arrive(bt.at[q, shard(3), REST_A], ag.at[q, 6])
            send(bt.at[q, shard(3), REST_A], bt.at[q, shard(2), REST_A], ag.at[q, 8], xp)
        else:
            arrive(bt.at[q, shard(1), REST_B], ag.at[q, 7])
            send(bt.at[q, shard(1), REST_B], bt.at[q, shard(2), REST_B], ag.at[q, 9], xm)

    def take_far(q):
        arrive(bt.at[q, shard(1), REST_A], ag.at[q, 10])
        arrive(bt.at[q, shard(3), REST_B], ag.at[q, 11])
        arrive(bt.at[q, shard(2), REST_A], ag.at[q, 8])
        arrive(bt.at[q, shard(2), REST_B], ag.at[q, 9])

    def product(q, i):
        if q == 0 and i == 0:
            load_b.wait()
        multiply(q, 1 - core if i < 2 else core, i % 2)
        if i == 1:
            swap(q)

    def multiply(q, which, i):
        start = pl.multiple_of(which * HALF + i * BLOCK, BLOCK)
        cb[q, which, :, i * BLOCK : (i + 1) * BLOCK] = lax.dot_general(
            bt[q], a[pl.ds(start, BLOCK), :], (((1,), (1,)), ((), ())), preferred_element_type=jnp.float32
        )

    def swap(q):
        send(cb.at[q, 1 - core], xb.at[q], ex.at[q], partner)

    def spot(q, delta):
        h = origin(q) // 4
        e = (z + NZ - h) % NZ
        j = ((e + delta + NZ) // 2 + NX - x) % NX
        return cb.at[q, core, pl.ds(pl.multiple_of(j * SHARD, SHARD), SHARD), :]

    def is_even(q):
        return (z + origin(q) // 4) % 2 == 0

    base = BASE

    def pass_on(q, src, slot, sem, dev):
        copy_of(src, rb.at[q, slot], ssem.at[base + 4 * q + sem], ch.at[q, slot], dev).start()

    def merge(q):
        arrive(xb.at[q], ex.at[q])
        cb[q, core] += xb[q]

    def stage1(q):
        even = is_even(q)

        @pl.when(even)
        def _():
            pass_on(q, spot(q, 4), 0, 0, ahead)

    def stage2(q):
        even = is_even(q)

        @pl.when(jnp.logical_not(even))
        def _():
            pass_on(q, spot(q, -3 * sigma), 1, 1, behind)
            arrive(rb.at[q, 0], ch.at[q, 0])
            here = spot(q, 3 * sigma)
            here[...] += rb[q, 0]
            pass_on(q, here, 0, 0, ahead)

    def stage3(q):
        even = is_even(q)

        @pl.when(even)
        def _():
            for slot, sign, dev in ((1, -1, behind), (0, 1, ahead)):
                arrive(rb.at[q, slot], ch.at[q, slot])
                here = spot(q, 2 * sign * sigma)
                here[...] += rb[q, slot]
                pass_on(q, here, 2 + slot, 1 + slot, dev)

    def stage4(q):
        even = is_even(q)

        @pl.when(jnp.logical_not(even))
        def _():
            for slot, sign, dev in ((1, -1, behind), (0, 1, ahead)):
                arrive(rb.at[q, 2 + slot], ch.at[q, 2 + slot])
                here = spot(q, sign * sigma)
                here[...] += rb[q, 2 + slot]
                pass_on(q, here, 2 + slot, 2 + slot, dev)

    def straight(q, src, slot, sem, dev):
        f = FAST.index(q)
        copy_of(src, fb.at[f, slot], ssem.at[base + 4 * q + sem], fch.at[f, slot], dev).start()

    def fast1(q):
        even = is_even(q)

        @pl.when(even)
        def _():
            straight(q, spot(q, 4), 0, 0, ahead)
            straight(q, spot(q, 2), 3, 1, along_z(2))
            straight(q, spot(q, -2), 4, 2, along_z(-2))

        @pl.when(jnp.logical_not(even))
        def _():
            straight(q, spot(q, -3 * sigma), 5 + (1 + sigma) // 2, 0, along_z(-3 * sigma))
            straight(q, spot(q, 1), 1, 1, along_z(1))
            straight(q, spot(q, -1), 2, 2, along_z(-1))

    def fast2(q):
        even = is_even(q)

        @pl.when(jnp.logical_not(even))
        def _():
            f = FAST.index(q)
            arrive(fb.at[f, 0], fch.at[f, 0])
            here = spot(q, 3 * sigma)
            here[...] += fb[f, 0]
            straight(q, here, 5 + (1 - sigma) // 2, 3, along_z(3 * sigma))

    def place(ref, index):
        columns = pl.ds(pl.multiple_of(core * HALF, HALF), HALF)
        return ref.at[index, :, columns]

    def finish(q):
        even = is_even(q)
        origin_y = origin(q)
        index = origin_y % 2
        mine = (origin_y // 2) % 2 == core

        @pl.when(even)
        def _():
            total = spot(q, 0)[...]
            if q in FAST:
                f = FAST.index(q)
                for slot in range(1, 7):
                    arrive(fb.at[f, slot], fch.at[f, slot])
                    total += fb[f, slot]
            else:
                for slot in (2, 3):
                    arrive(rb.at[q, slot], ch.at[q, slot])
                    total += rb[q, slot]
            total = total.astype(jnp.bfloat16)

            @pl.when(mine)
            def _():
                place(done, index)[...] = total

            @pl.when(jnp.logical_not(mine))
            def _():
                fin[index] = total
                copy_of(fin.at[index], place(done, index), fs.at[0, index], fs.at[1, index], partner).start()

    def mask_rows(part):
        if part == 0:
            load_a.wait()

        def apply_mask(i, carry):
            rows = pl.ds(pl.multiple_of(i * TILE, TILE), TILE)
            for k in range(DEPTH // TILE):
                cols = slice(k * TILE, (k + 1) * TILE)
                a[rows, cols] = jnp.where(mask[i, k] != 0, a[rows, cols], jnp.zeros((TILE, TILE), jnp.bfloat16))
            return carry

        lax.fori_loop(4 * part, 4 * part + 4, apply_mask, 0)

    for step, *args in (
        (own_rest_y,),
        (own_first_x,),
        (own_first_y,),
        (own_rest_x,),
        (mask_rows, 0),
        (gather, 1),
        (gather, 3),
        (take_rest, 2),
        (take_rest, 1),
        (take_first, 1, 0),
        (relay, 0, 3),
        (relay, 0, 1),
        (take_first, 2, 0),
        (gather_far,),
        (mask_rows, 1),
        (relay, 2, 1),
        (take_first, 2, 1),
        (relay, 2, 3),
        (relay, 1, 3),
        (relay, 1, 1),
        (take_first, 1, 3),
        (take_rest, 4),
        (take_first, 2, 3),
        (take_rest, 3),
        (take_first, 1, 1),
        (take_far, 0),
        (product, 0, 0),
        (product, 0, 1),
        (take_far, 2),
        (take_first, 2, 2),
        (product, 2, 0),
        (take_first, 1, 2),
        (take_first, 4, 0),
        (product, 0, 2),
        (product, 2, 1),
        (product, 0, 3),
        (take_first, 3, 0),
        (take_far, 1),
        (relay, 4, 3),
        (relay, 4, 1),
        (merge, 0),
        (product, 2, 2),
        (take_first, 4, 1),
        (take_rest, 6),
        (stage1, 0),
        (product, 2, 3),
        (product, 1, 0),
        (relay, 3, 1),
        (product, 1, 1),
        (relay, 3, 3),
        (product, 1, 2),
        (take_first, 4, 2),
        (merge, 2),
        (take_first, 4, 3),
        (take_rest, 5),
        (stage1, 2),
        (take_first, 3, 2),
        (take_first, 3, 3),
        (product, 1, 3),
        (take_far, 4),
        (product, 4, 0),
        (take_first, 3, 1),
        (merge, 1),
        (stage1, 1),
        (product, 4, 1),
        (relay, 6, 3),
        (take_first, 5, 0),
        (relay, 6, 1),
        (stage2, 0),
        (product, 4, 2),
        (take_rest_far, 6),
        (take_first, 6, 1),
        (product, 4, 3),
        (take_far, 3),
        (product, 3, 0),
        (product, 3, 1),
        (relay, 5, 1),
        (relay, 5, 3),
        (take_first, 6, 2),
        (product, 3, 2),
        (stage2, 2),
        (take_rest_far, 5),
        (product, 3, 3),
        (merge, 4),
        (merge, 3),
        (take_first, 5, 2),
        (take_first, 6, 3),
        (stage1, 4),
        (stage1, 3),
        (take_first, 6, 0),
        (stage2, 1),
        (take_far, 6),
        (product, 6, 0),
        (product, 6, 1),
        (take_first, 5, 3),
        (product, 6, 2),
        (stage3, 0),
        (product, 6, 3),
        (relay, 7, 1),
        (take_far, 5),
        (take_first, 5, 1),
        (product, 5, 0),
        (product, 5, 1),
        (relay, 7, 3),
        (merge, 6),
        (stage1, 6),
        (stage3, 2),
        (product, 5, 2),
        (product, 5, 3),
        (take_first, 7, 0),
        (merge, 5),
        (stage1, 5),
        (stage2, 3),
        (stage2, 4),
        (stage3, 1),
        (take_first, 7, 1),
        (stage2, 6),
        (take_first, 7, 2),
        (stage4, 0),
        (take_far, 7),
        (take_first, 7, 3),
        (product, 7, 0),
        (product, 7, 1),
        (stage2, 5),
        (product, 7, 2),
        (product, 7, 3),
        (merge, 7),
        (fast1, 7),
        (stage3, 4),
        (stage3, 3),
        (stage3, 5),
        (stage3, 6),
        (stage4, 2),
        (stage4, 1),
        (fast2, 7),
        (stage4, 4),
        (finish, 0),
        (stage4, 3),
        (stage4, 5),
        (stage4, 6),
        (finish, 7),
        (finish, 1),
        (finish, 2),
        (finish, 4),
        (finish, 3),
        (finish, 5),
        (finish, 6),
    ):
        step(*args)

    for index in range(2):
        half = pl.ds(pl.multiple_of((1 - core) * HALF, HALF), HALF)
        arrive(done.at[index, :, half], fs.at[1, index])
        copy_of(fin.at[index], place(done, index), fs.at[0, index], fs.at[1, index], partner).wait_send()
    for index in range(2):
        out[index * SHARD : (index + 1) * SHARD, :] = done[index]

    for copy in pending:
        copy.wait_send()
    for q in range(8):
        even = is_even(q)

        @pl.when(even)
        def _():
            for slot in range(3):
                copy_of(rb.at[q, 0], rb.at[q, 0], ssem.at[base + 4 * q + slot], ch.at[q, 0], partner).wait_send()

        @pl.when(jnp.logical_not(even))
        def _():
            for slot in range(4):
                copy_of(rb.at[q, 0], rb.at[q, 0], ssem.at[base + 4 * q + slot], ch.at[q, 0], partner).wait_send()


def per_device(amplitudes, integrals, tile_mask):
    result = pl.pallas_call(
        kernel,
        out_shape=jax.ShapeDtypeStruct((2 * SHARD, ROWS), jnp.bfloat16),
        in_specs=[
            pl.BlockSpec(memory_space=pl.ANY),
            pl.BlockSpec(memory_space=pl.ANY),
            pl.BlockSpec(memory_space=pltpu.SMEM),
        ],
        out_specs=pl.BlockSpec(memory_space=pltpu.VMEM),
        scratch_shapes=[
            pltpu.VMEM((ROWS, DEPTH), jnp.bfloat16),
            pltpu.VMEM((8, 4 * SHARD, DEPTH), jnp.bfloat16),
            pltpu.VMEM((8, 2, 4 * SHARD, HALF), jnp.float32),
            pltpu.VMEM((8, 4 * SHARD, HALF), jnp.float32),
            pltpu.VMEM((8, 4, SHARD, HALF), jnp.float32),
            pltpu.VMEM((len(FAST), 7, SHARD, HALF), jnp.float32),
            pltpu.VMEM((2, SHARD, HALF), jnp.bfloat16),
            pltpu.VMEM((2, SHARD, ROWS), jnp.bfloat16),
            pltpu.SemaphoreType.DMA((2,)),
            pltpu.SemaphoreType.DMA((N_SEND,)),
            pltpu.SemaphoreType.DMA((8, 12)),
            pltpu.SemaphoreType.DMA((8,)),
            pltpu.SemaphoreType.DMA((8, 4)),
            pltpu.SemaphoreType.DMA((len(FAST), 7)),
            pltpu.SemaphoreType.DMA((2, 2)),
        ],
        compiler_params=pltpu.CompilerParams(
            collective_id=0, has_side_effects=True, vmem_limit_bytes=60 * 1024 * 1024
        ),
    )(amplitudes, integrals.T, tile_mask)
    return result.T


def solution(mesh):
    placed = (P("row", "col"), P("col", "row"), P("row", "col"))
    return jax.shard_map(
        per_device, mesh=mesh, in_specs=placed, out_specs=P("row", "col"), check_vma=False
    )
```

time: 83.1 us -> 68.7 us (0.83); the launches traced: 81.9 us -> 68.6 us
  Pallas kernels: 80.3 us -> 67 us
    pallas_call x1, Pallas kernels: 80.3 us -> 67 us  [per_device(): pl.pallas_call(kernel, out_shape=jax.ShapeDtypeStruct((2 * SHARD, ROWS),...]
where the time goes in v2:
time: 68.7 us; the launch traced here: 68.6 us
  Pallas kernels  67 us (98%)
  local copies, waits for them, and re-layouts  1.57 us (2%)
    pallas_call x1, Pallas kernels, per_device(): pl.pallas_call(kernel, out_shape=jax.ShapeDtypeStruct((2 * SHARD, ROWS),...  67 us
    unnamed x1, local copies, waits for them, and re-layouts  1.57 us

profile of v2, /device:TPU:1, one launch (start us, length us, event | category | flops | bytes accessed | tf_op | source)
XLA Modules:
  0.0 68.6 jit_solution(15679504071743467398)
XLA Ops:
  0.0 67.0 %shard_map.37 = bf16[64,1024]{1,0:T(8,128)(2,1)} custom-call(bf16[1024,2048]{1,0:T(8,128)(2,1)} %a_hbm.1, bf16[32,2048]{1,0:T(8,128)(2,1)} %bitcast.3, s32[8,16]{1,0:T(8,128)} %mask.1), custom_call_target="tpu_custom_call" | custom-call | tf_op jit(solution)/shard_map/pallas_call | solution.py:489
  67.0 1.6 %copy.5 = bf16[1024,64]{0,1:T(8,128)(2,1)} copy(bf16[1024,64]{0,1:T(8,128)(2,1)} %bitcast.2) | data formatting | bytes 262144

commit v3 on v2

--- a/solution.py
+++ b/solution.py
@@ -12,6 +12,8 @@
 ROWS = 1024
 DEPTH = 2048
 HALF = ROWS // 2
+LEVELS = 32000.0
+CODED = SHARD * HALF // TILE + 16
 BLOCK = 256
 SPLIT = 768
 
@@ -23,14 +25,14 @@
 REST_B = slice((SPLIT + DEPTH) // 2, DEPTH)
 BASE = 100
 N_SEND = BASE + 32
-FAST = (7,)
+FAST = (6, 7)
 
 
 def shard(j):
     return slice(j * SHARD, (j + 1) * SHARD)
 
 
-def kernel(a_hbm, own, mask, out, a, bt, cb, xb, rb, fb, fin, done, lsem, ssem, ag, ex, ch, fch, fs):
+def kernel(a_hbm, own, mask, out, a, bt, cb, xb, eb, rb, fb, fin, done, lsem, ssem, ag, ex, ch, fch, fs):
     row, col = lax.axis_index("row"), lax.axis_index("col")
     x, y = row // NY, row % NY
     z, core = col // 2, col % 2
@@ -177,116 +179,133 @@
     def swap(q):
         send(cb.at[q, 1 - core], xb.at[q], ex.at[q], partner)
 
-    def spot(q, delta):
-        h = origin(q) // 4
+    def encode(values, ref):
+        parts = [values[:, m * TILE : (m + 1) * TILE].reshape(SHARD // 8, 8, TILE) for m in range(HALF // TILE)]
+        top = jnp.max(jnp.abs(parts[0]), axis=0)
+        for part in parts[1:]:
+            top = jnp.maximum(top, jnp.max(jnp.abs(part), axis=0))
+        power = jnp.ceil(jnp.log2(jnp.maximum(top, 1e-30)))
+        scale = (jnp.exp2(-power) * LEVELS)[None]
+        for m, part in enumerate(parts):
+            whole = jnp.round(part * scale).reshape(SHARD, TILE)
+            ref[m * SHARD : (m + 1) * SHARD, :] = whole.astype(jnp.int32).astype(jnp.int16)
+        both = jnp.concatenate([power, power], axis=0)
+        ref[CODED - 16 :, :] = both.astype(jnp.int32).astype(jnp.int16)
+
+    def decode(ref):
+        power = ref[CODED - 16 :, :].astype(jnp.int32).astype(jnp.float32)[:8]
+        step = (jnp.exp2(power) * (1.0 / LEVELS))[None]
+        parts = []
+        for m in range(HALF // TILE):
+            whole = ref[m * SHARD : (m + 1) * SHARD, :].astype(jnp.int32).astype(jnp.float32)
+            parts.append((whole.reshape(SHARD // 8, 8, TILE) * step).reshape(SHARD, TILE))
+        return jnp.concatenate(parts, axis=1)
+
+    evens, slots = [], []
+    for h in range(2):
         e = (z + NZ - h) % NZ
-        j = ((e + delta + NZ) // 2 + NX - x) % NX
+        evens.append(e % 2)
+        slots.append((e // 2 + NX - x) % NX)
+    halves = [origin(q) // 4 for q in range(8)]
+    parity = [evens[0] + (evens[1] - evens[0]) * h for h in halves]
+    slot0 = [slots[0] + (slots[1] - slots[0]) * h for h in halves]
+    plus3 = (3 * sigma + 1) // 2
+    minus3 = (1 - 3 * sigma) // 2
+
+    def at(q, steps):
+        j = (slot0[q] + steps + NX) % NX
         return cb.at[q, core, pl.ds(pl.multiple_of(j * SHARD, SHARD), SHARD), :]
 
+    base = BASE
+
     def is_even(q):
-        return (z + origin(q) // 4) % 2 == 0
-
-    base = BASE
-
-    def pass_on(q, src, slot, sem, dev):
-        copy_of(src, rb.at[q, slot], ssem.at[base + 4 * q + sem], ch.at[q, slot], dev).start()
+        return parity[q] == 0
+
+    def pass_on(q, values, slot, sem, dev):
+        encode(values, eb.at[q, sem])
+        copy_of(eb.at[q, sem], rb.at[q, slot], ssem.at[base + 4 * q + sem], ch.at[q, slot], dev).start()
 
     def merge(q):
         arrive(xb.at[q], ex.at[q])
         cb[q, core] += xb[q]
 
+    def add_in(q, steps, ref, sem):
+        arrive(ref, sem)
+        return at(q, steps)[...] + decode(ref)
+
     def stage1(q):
-        even = is_even(q)
-
-        @pl.when(even)
-        def _():
-            pass_on(q, spot(q, 4), 0, 0, ahead)
+        @pl.when(is_even(q))
+        def _():
+            pass_on(q, at(q, 2)[...], 0, 0, ahead)
+
+        @pl.when(jnp.logical_not(is_even(q)))
+        def _():
+            pass_on(q, at(q, minus3)[...], 1, 1, behind)
 
     def stage2(q):
-        even = is_even(q)
-
-        @pl.when(jnp.logical_not(even))
-        def _():
-            pass_on(q, spot(q, -3 * sigma), 1, 1, behind)
-            arrive(rb.at[q, 0], ch.at[q, 0])
-            here = spot(q, 3 * sigma)
-            here[...] += rb[q, 0]
-            pass_on(q, here, 0, 0, ahead)
+        @pl.when(jnp.logical_not(is_even(q)))
+        def _():
+            pass_on(q, add_in(q, plus3, rb.at[q, 0], ch.at[q, 0]), 0, 0, ahead)
 
     def stage3(q):
-        even = is_even(q)
-
-        @pl.when(even)
-        def _():
-            for slot, sign, dev in ((1, -1, behind), (0, 1, ahead)):
-                arrive(rb.at[q, slot], ch.at[q, slot])
-                here = spot(q, 2 * sign * sigma)
-                here[...] += rb[q, slot]
-                pass_on(q, here, 2 + slot, 1 + slot, dev)
+        @pl.when(is_even(q))
+        def _():
+            for slot, steps, dev in ((1, -sigma, behind), (0, sigma, ahead)):
+                pass_on(q, add_in(q, steps, rb.at[q, slot], ch.at[q, slot]), 2 + slot, 1 + slot, dev)
+
+    up, down = (1 + sigma) // 2, (1 - sigma) // 2
 
     def stage4(q):
-        even = is_even(q)
-
-        @pl.when(jnp.logical_not(even))
-        def _():
-            for slot, sign, dev in ((1, -1, behind), (0, 1, ahead)):
-                arrive(rb.at[q, 2 + slot], ch.at[q, 2 + slot])
-                here = spot(q, sign * sigma)
-                here[...] += rb[q, 2 + slot]
-                pass_on(q, here, 2 + slot, 2 + slot, dev)
-
-    def straight(q, src, slot, sem, dev):
+        @pl.when(jnp.logical_not(is_even(q)))
+        def _():
+            for slot, steps, dev in ((1, down, behind), (0, up, ahead)):
+                pass_on(q, add_in(q, steps, rb.at[q, 2 + slot], ch.at[q, 2 + slot]), 2 + slot, 2 + slot, dev)
+
+    def straight(q, values, slot, sem, dev):
         f = FAST.index(q)
-        copy_of(src, fb.at[f, slot], ssem.at[base + 4 * q + sem], fch.at[f, slot], dev).start()
+        encode(values, eb.at[q, sem])
+        copy_of(eb.at[q, sem], fb.at[f, slot], ssem.at[base + 4 * q + sem], fch.at[f, slot], dev).start()
 
     def fast1(q):
-        even = is_even(q)
-
-        @pl.when(even)
-        def _():
-            straight(q, spot(q, 4), 0, 0, ahead)
-            straight(q, spot(q, 2), 3, 1, along_z(2))
-            straight(q, spot(q, -2), 4, 2, along_z(-2))
-
-        @pl.when(jnp.logical_not(even))
-        def _():
-            straight(q, spot(q, -3 * sigma), 5 + (1 + sigma) // 2, 0, along_z(-3 * sigma))
-            straight(q, spot(q, 1), 1, 1, along_z(1))
-            straight(q, spot(q, -1), 2, 2, along_z(-1))
+        @pl.when(is_even(q))
+        def _():
+            straight(q, at(q, 2)[...], 0, 0, ahead)
+            straight(q, at(q, 1)[...], 3, 1, along_z(2))
+            straight(q, at(q, -1)[...], 4, 2, along_z(-2))
+
+        @pl.when(jnp.logical_not(is_even(q)))
+        def _():
+            straight(q, at(q, minus3)[...], 5 + up, 0, along_z(-3 * sigma))
+            straight(q, at(q, 1)[...], 1, 1, along_z(1))
+            straight(q, at(q, 0)[...], 2, 2, along_z(-1))
 
     def fast2(q):
-        even = is_even(q)
-
-        @pl.when(jnp.logical_not(even))
+        @pl.when(jnp.logical_not(is_even(q)))
         def _():
             f = FAST.index(q)
-            arrive(fb.at[f, 0], fch.at[f, 0])
-            here = spot(q, 3 * sigma)
-            here[...] += fb[f, 0]
-            straight(q, here, 5 + (1 - sigma) // 2, 3, along_z(3 * sigma))
+            straight(q, add_in(q, plus3, fb.at[f, 0], fch.at[f, 0]), 5 + down, 3, along_z(3 * sigma))
 
     def place(ref, index):
         columns = pl.ds(pl.multiple_of(core * HALF, HALF), HALF)
         return ref.at[index, :, columns]
 
     def finish(q):
-        even = is_even(q)
         origin_y = origin(q)
         index = origin_y % 2
         mine = (origin_y // 2) % 2 == core
 
-        @pl.when(even)
-        def _():
-            total = spot(q, 0)[...]
+        @pl.when(is_even(q))
+        def _():
+            total = at(q, 0)[...]
             if q in FAST:
                 f = FAST.index(q)
                 for slot in range(1, 7):
                     arrive(fb.at[f, slot], fch.at[f, slot])
-                    total += fb[f, slot]
+                    total += decode(fb.at[f, slot])
             else:
                 for slot in (2, 3):
                     arrive(rb.at[q, slot], ch.at[q, slot])
-                    total += rb[q, slot]
+                    total += decode(rb.at[q, slot])
             total = total.astype(jnp.bfloat16)
 
             @pl.when(mine)
@@ -314,151 +333,149 @@
     for step, *args in (
         (own_rest_y,),
         (own_first_x,),
+        (own_rest_x,),
         (own_first_y,),
-        (own_rest_x,),
-        (mask_rows, 0),
+        (gather, 3),
         (gather, 1),
-        (gather, 3),
-        (take_rest, 2),
         (take_rest, 1),
-        (take_first, 1, 0),
         (relay, 0, 3),
         (relay, 0, 1),
-        (take_first, 2, 0),
+        (mask_rows, 0),
+        (take_rest, 2),
         (gather_far,),
         (mask_rows, 1),
-        (relay, 2, 1),
-        (take_first, 2, 1),
-        (relay, 2, 3),
-        (relay, 1, 3),
         (relay, 1, 1),
         (take_first, 1, 3),
-        (take_rest, 4),
-        (take_first, 2, 3),
-        (take_rest, 3),
+        (take_first, 2, 1),
+        (relay, 1, 3),
+        (take_first, 2, 0),
         (take_first, 1, 1),
         (take_far, 0),
+        (take_first, 2, 3),
         (product, 0, 0),
+        (take_rest, 4),
+        (relay, 2, 1),
+        (relay, 2, 3),
+        (take_rest, 3),
         (product, 0, 1),
+        (product, 0, 2),
+        (take_first, 2, 2),
+        (product, 0, 3),
+        (take_first, 1, 0),
+        (take_far, 1),
+        (take_first, 1, 2),
+        (merge, 0),
+        (product, 1, 0),
+        (product, 1, 1),
+        (product, 1, 2),
+        (take_first, 4, 1),
+        (relay, 4, 3),
+        (stage1, 0),
+        (take_first, 3, 1),
+        (relay, 4, 1),
+        (product, 1, 3),
+        (take_first, 3, 3),
+        (take_first, 4, 3),
+        (merge, 1),
+        (take_rest, 5),
+        (stage1, 1),
+        (take_first, 4, 0),
         (take_far, 2),
-        (take_first, 2, 2),
         (product, 2, 0),
-        (take_first, 1, 2),
-        (take_first, 4, 0),
-        (product, 0, 2),
         (product, 2, 1),
-        (product, 0, 3),
+        (relay, 3, 3),
         (take_first, 3, 0),
-        (take_far, 1),
-        (relay, 4, 3),
-        (relay, 4, 1),
-        (merge, 0),
+        (relay, 3, 1),
+        (take_rest, 6),
         (product, 2, 2),
-        (take_first, 4, 1),
-        (take_rest, 6),
-        (stage1, 0),
+        (take_first, 4, 2),
         (product, 2, 3),
-        (product, 1, 0),
-        (relay, 3, 1),
-        (product, 1, 1),
-        (relay, 3, 3),
-        (product, 1, 2),
-        (take_first, 4, 2),
         (merge, 2),
-        (take_first, 4, 3),
-        (take_rest, 5),
-        (stage1, 2),
-        (take_first, 3, 2),
-        (take_first, 3, 3),
-        (product, 1, 3),
         (take_far, 4),
         (product, 4, 0),
-        (take_first, 3, 1),
-        (merge, 1),
-        (stage1, 1),
+        (stage1, 2),
         (product, 4, 1),
+        (relay, 5, 1),
+        (take_first, 6, 1),
+        (take_first, 3, 2),
+        (relay, 5, 3),
+        (product, 4, 2),
+        (take_rest_far, 5),
+        (product, 4, 3),
+        (merge, 4),
+        (take_far, 3),
+        (stage2, 1),
+        (product, 3, 0),
+        (take_rest_far, 6),
+        (product, 3, 1),
         (relay, 6, 3),
+        (relay, 6, 1),
+        (product, 3, 2),
+        (take_first, 6, 0),
+        (take_first, 5, 3),
+        (stage1, 4),
+        (product, 3, 3),
+        (merge, 3),
+        (take_first, 7, 1),
+        (take_far, 5),
+        (stage1, 3),
         (take_first, 5, 0),
-        (relay, 6, 1),
+        (take_first, 5, 2),
+        (take_first, 5, 1),
+        (product, 5, 0),
+        (stage2, 2),
+        (product, 5, 1),
         (stage2, 0),
-        (product, 4, 2),
-        (take_rest_far, 6),
-        (take_first, 6, 1),
-        (product, 4, 3),
-        (take_far, 3),
-        (product, 3, 0),
-        (product, 3, 1),
-        (relay, 5, 1),
-        (relay, 5, 3),
+        (product, 5, 2),
+        (relay, 7, 3),
+        (relay, 7, 1),
+        (product, 5, 3),
         (take_first, 6, 2),
-        (product, 3, 2),
-        (stage2, 2),
-        (take_rest_far, 5),
-        (product, 3, 3),
-        (merge, 4),
-        (merge, 3),
-        (take_first, 5, 2),
+        (merge, 5),
+        (stage1, 5),
+        (stage3, 1),
         (take_first, 6, 3),
-        (stage1, 4),
-        (stage1, 3),
-        (take_first, 6, 0),
-        (stage2, 1),
         (take_far, 6),
         (product, 6, 0),
         (product, 6, 1),
-        (take_first, 5, 3),
         (product, 6, 2),
+        (take_first, 7, 0),
+        (stage2, 4),
+        (stage2, 3),
+        (take_first, 7, 3),
+        (stage3, 2),
+        (product, 6, 3),
         (stage3, 0),
-        (product, 6, 3),
-        (relay, 7, 1),
-        (take_far, 5),
-        (take_first, 5, 1),
-        (product, 5, 0),
-        (product, 5, 1),
-        (relay, 7, 3),
         (merge, 6),
-        (stage1, 6),
-        (stage3, 2),
-        (product, 5, 2),
-        (product, 5, 3),
-        (take_first, 7, 0),
-        (merge, 5),
-        (stage1, 5),
-        (stage2, 3),
-        (stage2, 4),
-        (stage3, 1),
-        (take_first, 7, 1),
-        (stage2, 6),
+        (stage2, 5),
+        (take_far, 7),
+        (fast1, 6),
         (take_first, 7, 2),
-        (stage4, 0),
-        (take_far, 7),
-        (take_first, 7, 3),
         (product, 7, 0),
         (product, 7, 1),
-        (stage2, 5),
         (product, 7, 2),
+        (stage3, 4),
+        (stage3, 3),
         (product, 7, 3),
         (merge, 7),
         (fast1, 7),
-        (stage3, 4),
-        (stage3, 3),
+        (stage4, 1),
         (stage3, 5),
-        (stage3, 6),
+        (fast2, 6),
+        (fast2, 7),
+        (stage4, 0),
+        (stage4, 3),
+        (stage4, 4),
         (stage4, 2),
-        (stage4, 1),
-        (fast2, 7),
-        (stage4, 4),
-        (finish, 0),
-        (stage4, 3),
+        (finish, 1),
         (stage4, 5),
-        (stage4, 6),
-        (finish, 7),
-        (finish, 1),
-        (finish, 2),
+        (finish, 6),
         (finish, 4),
         (finish, 3),
+        (finish, 2),
+        (finish, 0),
         (finish, 5),
-        (finish, 6),
+        (finish, 7),
     ):
         step(*args)
 
@@ -472,14 +489,12 @@
     for copy in pending:
         copy.wait_send()
     for q in range(8):
-        even = is_even(q)
-
-        @pl.when(even)
+        @pl.when(is_even(q))
         def _():
             for slot in range(3):
                 copy_of(rb.at[q, 0], rb.at[q, 0], ssem.at[base + 4 * q + slot], ch.at[q, 0], partner).wait_send()
 
-        @pl.when(jnp.logical_not(even))
+        @pl.when(jnp.logical_not(is_even(q)))
         def _():
             for slot in range(4):
                 copy_of(rb.at[q, 0], rb.at[q, 0], ssem.at[base + 4 * q + slot], ch.at[q, 0], partner).wait_send()
@@ -500,8 +515,9 @@
             pltpu.VMEM((8, 4 * SHARD, DEPTH), jnp.bfloat16),
             pltpu.VMEM((8, 2, 4 * SHARD, HALF), jnp.float32),
             pltpu.VMEM((8, 4 * SHARD, HALF), jnp.float32),
-            pltpu.VMEM((8, 4, SHARD, HALF), jnp.float32),
-            pltpu.VMEM((len(FAST), 7, SHARD, HALF), jnp.float32),
+            pltpu.VMEM((8, 4, CODED, TILE), jnp.int16),
+            pltpu.VMEM((8, 4, CODED, TILE), jnp.int16),
+            pltpu.VMEM((len(FAST), 7, CODED, TILE), jnp.int16),
             pltpu.VMEM((2, SHARD, HALF), jnp.bfloat16),
             pltpu.VMEM((2, SHARD, ROWS), jnp.bfloat16),
             pltpu.SemaphoreType.DMA((2,)),

time: 68.7 us -> 62.6 us (0.911)
  Pallas kernels: 67 us -> 60.9 us
    pallas_call x1, Pallas kernels: 67 us -> 60.9 us  [per_device(): pl.pallas_call(kernel, out_shape=jax.ShapeDtypeStruct((2 * SHARD, ROWS),...]
where the time goes in v3:
time: 62.6 us; the launch traced here: 62.5 us
  Pallas kernels  60.9 us (97%)
  local copies, waits for them, and re-layouts  1.57 us (3%)
    pallas_call x1, Pallas kernels, per_device(): pl.pallas_call(kernel, out_shape=jax.ShapeDtypeStruct((2 * SHARD, ROWS),...  60.9 us
    unnamed x1, local copies, waits for them, and re-layouts  1.57 us

profile of v3, /device:TPU:1, one launch (start us, length us, event | category | flops | bytes accessed | tf_op | source)
XLA Modules:
  0.0 62.5 jit_solution(15358469707442341647)
XLA Ops:
  0.0 60.9 %shard_map.37 = bf16[64,1024]{1,0:T(8,128)(2,1)} custom-call(bf16[1024,2048]{1,0:T(8,128)(2,1)} %a_hbm.1, bf16[32,2048]{1,0:T(8,128)(2,1)} %bitcast.3, s32[8,16]{1,0:T(8,128)} %mask.1), custom_call_target="tpu_custom_call" | custom-call | tf_op jit(solution)/shard_map/pallas_call | solution.py:504
  60.9 1.6 %copy.5 = bf16[1024,64]{0,1:T(8,128)(2,1)} copy(bf16[1024,64]{0,1:T(8,128)(2,1)} %bitcast.2) | data formatting | bytes 262144

commit v4 on v3

--- a/solution.py
+++ b/solution.py
@@ -25,7 +25,7 @@
 REST_B = slice((SPLIT + DEPTH) // 2, DEPTH)
 BASE = 100
 N_SEND = BASE + 32
-FAST = (6, 7)
+FAST = (7,)
 
 
 def shard(j):
@@ -168,13 +168,20 @@
             load_b.wait()
         multiply(q, 1 - core if i < 2 else core, i % 2)
         if i == 1:
-            swap(q)
+            for row_slot in (q,) if q in (0, 7) else (q, q + 1):
+                swap(row_slot)
 
     def multiply(q, which, i):
         start = pl.multiple_of(which * HALF + i * BLOCK, BLOCK)
-        cb[q, which, :, i * BLOCK : (i + 1) * BLOCK] = lax.dot_general(
-            bt[q], a[pl.ds(start, BLOCK), :], (((1,), (1,)), ((), ())), preferred_element_type=jnp.float32
+        n = 1 if q in (0, 7) else 2
+        sums = lax.dot_general(
+            bt[q : q + n].reshape(n * 4 * SHARD, DEPTH),
+            a[pl.ds(start, BLOCK), :],
+            (((1,), (1,)), ((), ())),
+            preferred_element_type=jnp.float32,
         )
+        for r in range(n):
+            cb[q + r, which, :, i * BLOCK : (i + 1) * BLOCK] = sums[r * 4 * SHARD : (r + 1) * 4 * SHARD]
 
     def swap(q):
         send(cb.at[q, 1 - core], xb.at[q], ex.at[q], partner)
@@ -332,150 +339,140 @@
 
     for step, *args in (
         (own_rest_y,),
+        (own_rest_x,),
+        (mask_rows, 0),
+        (own_first_y,),
         (own_first_x,),
-        (own_rest_x,),
-        (own_first_y,),
-        (gather, 3),
-        (gather, 1),
-        (take_rest, 1),
         (relay, 0, 3),
         (relay, 0, 1),
-        (mask_rows, 0),
         (take_rest, 2),
+        (take_rest, 1),
+        (gather, 1),
+        (gather, 3),
+        (relay, 2, 3),
+        (take_first, 1, 0),
+        (relay, 2, 1),
+        (take_rest, 4),
+        (take_rest, 3),
+        (take_far, 0),
+        (take_first, 2, 1),
+        (mask_rows, 1),
         (gather_far,),
-        (mask_rows, 1),
+        (product, 0, 0),
+        (take_first, 1, 1),
+        (take_first, 2, 3),
+        (product, 0, 1),
         (relay, 1, 1),
+        (take_first, 2, 0),
+        (take_far, 2),
+        (relay, 1, 3),
         (take_first, 1, 3),
-        (take_first, 2, 1),
-        (relay, 1, 3),
-        (take_first, 2, 0),
-        (take_first, 1, 1),
-        (take_far, 0),
-        (take_first, 2, 3),
-        (product, 0, 0),
-        (take_rest, 4),
-        (relay, 2, 1),
-        (relay, 2, 3),
-        (take_rest, 3),
-        (product, 0, 1),
         (product, 0, 2),
+        (relay, 4, 1),
+        (relay, 4, 3),
+        (product, 0, 3),
+        (take_rest, 5),
+        (relay, 3, 3),
+        (merge, 0),
+        (relay, 3, 1),
+        (take_rest, 6),
+        (take_first, 1, 2),
+        (stage1, 0),
         (take_first, 2, 2),
-        (product, 0, 3),
-        (take_first, 1, 0),
+        (take_first, 4, 1),
+        (take_first, 3, 1),
         (take_far, 1),
-        (take_first, 1, 2),
-        (merge, 0),
         (product, 1, 0),
         (product, 1, 1),
-        (product, 1, 2),
-        (take_first, 4, 1),
-        (relay, 4, 3),
-        (stage1, 0),
-        (take_first, 3, 1),
-        (relay, 4, 1),
-        (product, 1, 3),
         (take_first, 3, 3),
         (take_first, 4, 3),
+        (product, 1, 2),
+        (take_first, 4, 0),
+        (take_first, 3, 0),
+        (product, 1, 3),
         (merge, 1),
-        (take_rest, 5),
+        (take_rest_far, 5),
         (stage1, 1),
-        (take_first, 4, 0),
-        (take_far, 2),
-        (product, 2, 0),
-        (product, 2, 1),
-        (relay, 3, 3),
-        (take_first, 3, 0),
-        (relay, 3, 1),
-        (take_rest, 6),
-        (product, 2, 2),
+        (merge, 2),
+        (stage2, 0),
+        (take_far, 4),
+        (relay, 5, 1),
         (take_first, 4, 2),
-        (product, 2, 3),
-        (merge, 2),
-        (take_far, 4),
-        (product, 4, 0),
+        (relay, 5, 3),
         (stage1, 2),
-        (product, 4, 1),
-        (relay, 5, 1),
-        (take_first, 6, 1),
+        (take_far, 3),
         (take_first, 3, 2),
-        (relay, 5, 3),
-        (product, 4, 2),
-        (take_rest_far, 5),
-        (product, 4, 3),
-        (merge, 4),
-        (take_far, 3),
-        (stage2, 1),
         (product, 3, 0),
-        (take_rest_far, 6),
-        (product, 3, 1),
         (relay, 6, 3),
         (relay, 6, 1),
+        (product, 3, 1),
+        (take_rest_far, 6),
         (product, 3, 2),
-        (take_first, 6, 0),
         (take_first, 5, 3),
-        (stage1, 4),
         (product, 3, 3),
         (merge, 3),
-        (take_first, 7, 1),
+        (stage2, 1),
+        (take_first, 6, 1),
+        (merge, 4),
+        (stage3, 0),
+        (take_first, 5, 0),
         (take_far, 5),
+        (take_first, 6, 0),
+        (stage1, 4),
         (stage1, 3),
-        (take_first, 5, 0),
         (take_first, 5, 2),
+        (take_first, 6, 2),
+        (stage2, 2),
+        (take_far, 6),
         (take_first, 5, 1),
+        (take_first, 6, 3),
         (product, 5, 0),
-        (stage2, 2),
         (product, 5, 1),
-        (stage2, 0),
-        (product, 5, 2),
         (relay, 7, 3),
         (relay, 7, 1),
+        (product, 5, 2),
         (product, 5, 3),
-        (take_first, 6, 2),
         (merge, 5),
         (stage1, 5),
+        (merge, 6),
         (stage3, 1),
-        (take_first, 6, 3),
-        (take_far, 6),
-        (product, 6, 0),
-        (product, 6, 1),
-        (product, 6, 2),
+        (stage1, 6),
+        (stage4, 0),
         (take_first, 7, 0),
+        (take_first, 7, 1),
+        (take_first, 7, 2),
+        (stage2, 3),
         (stage2, 4),
-        (stage2, 3),
         (take_first, 7, 3),
         (stage3, 2),
-        (product, 6, 3),
-        (stage3, 0),
-        (merge, 6),
-        (stage2, 5),
         (take_far, 7),
-        (fast1, 6),
-        (take_first, 7, 2),
         (product, 7, 0),
         (product, 7, 1),
         (product, 7, 2),
+        (stage2, 5),
+        (product, 7, 3),
+        (stage2, 6),
+        (merge, 7),
+        (fast1, 7),
         (stage3, 4),
         (stage3, 3),
-        (product, 7, 3),
-        (merge, 7),
-        (fast1, 7),
+        (stage3, 5),
+        (stage3, 6),
+        (fast2, 7),
+        (stage4, 2),
         (stage4, 1),
-        (stage3, 5),
-        (fast2, 6),
-        (fast2, 7),
-        (stage4, 0),
+        (stage4, 4),
         (stage4, 3),
-        (stage4, 4),
-        (stage4, 2),
+        (stage4, 5),
+        (stage4, 6),
+        (finish, 2),
+        (finish, 0),
         (finish, 1),
-        (stage4, 5),
-        (finish, 6),
         (finish, 4),
         (finish, 3),
-        (finish, 2),
-        (finish, 0),
+        (finish, 7),
         (finish, 5),
-        (finish, 7),
+        (finish, 6),
     ):
         step(*args)
 

time: 62.6 us -> 62.4 us (level)
  no operation moved by 1% of the time
where the time goes in v4:
time: 62.4 us; the launch traced here: 62.3 us
  Pallas kernels  60.7 us (97%)
  local copies, waits for them, and re-layouts  1.57 us (3%)
    pallas_call x1, Pallas kernels, per_device(): pl.pallas_call(kernel, out_shape=jax.ShapeDtypeStruct((2 * SHARD, ROWS),...  60.7 us
    unnamed x1, local copies, waits for them, and re-layouts  1.57 us

profile of v4, /device:TPU:1, one launch (start us, length us, event | category | flops | bytes accessed | tf_op | source)
XLA Modules:
  0.0 62.3 jit_solution(6478385499383208121)
XLA Ops:
  0.0 60.7 %shard_map.37 = bf16[64,1024]{1,0:T(8,128)(2,1)} custom-call(bf16[1024,2048]{1,0:T(8,128)(2,1)} %a_hbm.1, bf16[32,2048]{1,0:T(8,128)(2,1)} %bitcast.3, s32[8,16]{1,0:T(8,128)} %mask.1), custom_call_target="tpu_custom_call" | custom-call | tf_op jit(solution)/shard_map/pallas_call | solution.py:501
  60.7 1.6 %copy.5 = bf16[1024,64]{0,1:T(8,128)(2,1)} copy(bf16[1024,64]{0,1:T(8,128)(2,1)} %bitcast.2) | data formatting | bytes 262144

commit v5 on v4

--- a/solution.py
+++ b/solution.py
@@ -497,6 +497,10 @@
                 copy_of(rb.at[q, 0], rb.at[q, 0], ssem.at[base + 4 * q + slot], ch.at[q, 0], partner).wait_send()
 
 
+def hand_over(sums, out):
+    out[...] = sums[...]
+
+
 def per_device(amplitudes, integrals, tile_mask):
     result = pl.pallas_call(
         kernel,
@@ -529,7 +533,12 @@
             collective_id=0, has_side_effects=True, vmem_limit_bytes=60 * 1024 * 1024
         ),
     )(amplitudes, integrals.T, tile_mask)
-    return result.T
+    return pl.pallas_call(
+        hand_over,
+        out_shape=jax.ShapeDtypeStruct(result.shape, result.dtype),
+        in_specs=[pl.BlockSpec(memory_space=pltpu.VMEM)],
+        out_specs=pl.BlockSpec(memory_space=pltpu.VMEM),
+    )(result).T
 
 
 def solution(mesh):

time: 62.4 us -> 62.4 us (level)
  Pallas kernels: 60.7 us -> 62.3 us
  local copies, waits for them, and re-layouts: 1.57 us -> 0 us
    pallas_call x0 -> x1, Pallas kernels: none -> 1.57 us  [per_device(): pl.pallas_call(hand_over, out_shape=jax.ShapeDtypeStruct(result.shape, re...]
    unnamed x1 -> x0, local copies, waits for them, and re-layouts: 1.57 us -> none
where the time goes in v5:
time: 62.4 us; the launch traced here: 62.3 us
  Pallas kernels  62.3 us (100%)
    pallas_call x1, Pallas kernels, per_device(): pl.pallas_call(kernel, out_shape=jax.ShapeDtypeStruct((2 * SHARD, ROWS),...  60.7 us
    pallas_call x1, Pallas kernels, per_device(): pl.pallas_call(hand_over, out_shape=jax.ShapeDtypeStruct(result.shape, re...  1.57 us

profile of v5, /device:TPU:1, one launch (start us, length us, event | category | flops | bytes accessed | tf_op | source)
XLA Modules:
  0.0 62.3 jit_solution(16517528391750249964)
XLA Ops:
  0.0 60.7 %shard_map.37.sums = bf16[64,1024]{1,0:T(8,128)(2,1)} custom-call(bf16[1024,2048]{1,0:T(8,128)(2,1)} %a_hbm.1, bf16[32,2048]{1,0:T(8,128)(2,1)} %bitcast.2, s32[8,16]{1,0:T(8,128)} %mask.1), custom_call_target="tpu_custom_call" | custom-call | tf_op jit(solution)/shard_map/pallas_call | solution.py:505
  60.7 1.6 %shard_map.38 = bf16[64,1024]{1,0:T(8,128)(2,1)} custom-call(bf16[64,1024]{1,0:T(8,128)(2,1)} %shard_map.37.sums), custom_call_target="tpu_custom_call" | custom-call | tf_op jit(solution)/shard_map/pallas_call | solution.py:536

commit v6 on v5

--- a/solution.py
+++ b/solution.py
@@ -25,7 +25,7 @@
 REST_B = slice((SPLIT + DEPTH) // 2, DEPTH)
 BASE = 100
 N_SEND = BASE + 32
-FAST = (7,)
+FAST = (6, 7)
 
 
 def shard(j):
@@ -338,141 +338,139 @@
         lax.fori_loop(4 * part, 4 * part + 4, apply_mask, 0)
 
     for step, *args in (
+        (own_first_x,),
         (own_rest_y,),
+        (own_first_y,),
         (own_rest_x,),
-        (mask_rows, 0),
-        (own_first_y,),
-        (own_first_x,),
+        (gather, 3),
+        (gather, 1),
         (relay, 0, 3),
         (relay, 0, 1),
         (take_rest, 2),
+        (mask_rows, 0),
         (take_rest, 1),
-        (gather, 1),
-        (gather, 3),
+        (gather_far,),
+        (take_first, 2, 3),
+        (take_first, 1, 3),
+        (mask_rows, 1),
         (relay, 2, 3),
-        (take_first, 1, 0),
         (relay, 2, 1),
         (take_rest, 4),
         (take_rest, 3),
+        (take_first, 1, 0),
+        (take_first, 2, 1),
+        (relay, 1, 3),
+        (relay, 1, 1),
+        (take_first, 2, 2),
+        (take_first, 3, 3),
         (take_far, 0),
-        (take_first, 2, 1),
-        (mask_rows, 1),
-        (gather_far,),
+        (take_first, 1, 2),
+        (take_first, 4, 3),
         (product, 0, 0),
+        (product, 0, 1),
+        (product, 0, 2),
+        (relay, 4, 3),
+        (relay, 4, 1),
+        (take_rest, 6),
+        (take_far, 2),
         (take_first, 1, 1),
-        (take_first, 2, 3),
-        (product, 0, 1),
-        (relay, 1, 1),
+        (product, 0, 3),
+        (merge, 0),
         (take_first, 2, 0),
-        (take_far, 2),
-        (relay, 1, 3),
-        (take_first, 1, 3),
-        (product, 0, 2),
-        (relay, 4, 1),
-        (relay, 4, 3),
-        (product, 0, 3),
+        (relay, 3, 3),
+        (relay, 3, 1),
         (take_rest, 5),
-        (relay, 3, 3),
-        (merge, 0),
-        (relay, 3, 1),
-        (take_rest, 6),
-        (take_first, 1, 2),
         (stage1, 0),
-        (take_first, 2, 2),
+        (take_first, 3, 0),
+        (take_far, 1),
         (take_first, 4, 1),
+        (product, 1, 0),
+        (take_first, 4, 2),
+        (take_first, 6, 3),
+        (product, 1, 1),
+        (take_first, 3, 2),
+        (product, 1, 2),
+        (take_rest_far, 6),
+        (take_first, 5, 3),
+        (relay, 6, 1),
+        (product, 1, 3),
+        (relay, 6, 3),
         (take_first, 3, 1),
-        (take_far, 1),
-        (product, 1, 0),
-        (product, 1, 1),
-        (take_first, 3, 3),
-        (take_first, 4, 3),
-        (product, 1, 2),
-        (take_first, 4, 0),
-        (take_first, 3, 0),
-        (product, 1, 3),
         (merge, 1),
-        (take_rest_far, 5),
         (stage1, 1),
         (merge, 2),
+        (take_first, 4, 0),
+        (stage1, 2),
+        (take_rest_far, 5),
         (stage2, 0),
         (take_far, 4),
+        (relay, 5, 3),
+        (take_far, 3),
         (relay, 5, 1),
-        (take_first, 4, 2),
-        (relay, 5, 3),
-        (stage1, 2),
-        (take_far, 3),
-        (take_first, 3, 2),
         (product, 3, 0),
-        (relay, 6, 3),
-        (relay, 6, 1),
         (product, 3, 1),
-        (take_rest_far, 6),
+        (take_first, 6, 1),
         (product, 3, 2),
-        (take_first, 5, 3),
         (product, 3, 3),
         (merge, 3),
         (stage2, 1),
-        (take_first, 6, 1),
         (merge, 4),
+        (take_first, 7, 3),
+        (take_first, 5, 0),
+        (stage1, 3),
+        (stage1, 4),
+        (take_first, 6, 0),
+        (take_first, 5, 2),
+        (take_first, 5, 1),
+        (take_far, 6),
+        (stage2, 2),
+        (relay, 7, 3),
+        (relay, 7, 1),
         (stage3, 0),
-        (take_first, 5, 0),
+        (take_first, 6, 2),
         (take_far, 5),
-        (take_first, 6, 0),
-        (stage1, 4),
-        (stage1, 3),
-        (take_first, 5, 2),
-        (take_first, 6, 2),
-        (stage2, 2),
-        (take_far, 6),
-        (take_first, 5, 1),
-        (take_first, 6, 3),
         (product, 5, 0),
         (product, 5, 1),
-        (relay, 7, 3),
-        (relay, 7, 1),
         (product, 5, 2),
         (product, 5, 3),
         (merge, 5),
         (stage1, 5),
         (merge, 6),
         (stage3, 1),
-        (stage1, 6),
-        (stage4, 0),
+        (take_first, 7, 1),
+        (fast1, 6),
+        (take_first, 7, 2),
+        (take_far, 7),
         (take_first, 7, 0),
-        (take_first, 7, 1),
-        (take_first, 7, 2),
-        (stage2, 3),
-        (stage2, 4),
-        (take_first, 7, 3),
-        (stage3, 2),
-        (take_far, 7),
         (product, 7, 0),
         (product, 7, 1),
+        (stage2, 4),
+        (stage2, 3),
         (product, 7, 2),
+        (product, 7, 3),
         (stage2, 5),
-        (product, 7, 3),
-        (stage2, 6),
         (merge, 7),
         (fast1, 7),
+        (fast2, 6),
+        (stage3, 2),
         (stage3, 4),
         (stage3, 3),
         (stage3, 5),
-        (stage3, 6),
         (fast2, 7),
+        (stage4, 1),
+        (stage4, 0),
         (stage4, 2),
-        (stage4, 1),
         (stage4, 4),
         (stage4, 3),
         (stage4, 5),
-        (stage4, 6),
-        (finish, 2),
+        (finish, 6),
         (finish, 0),
         (finish, 1),
+        (finish, 2),
+        (finish, 7),
+        (finish, 3),
         (finish, 4),
-        (finish, 3),
-        (finish, 7),
         (finish, 5),
-        (finish, 6),
     ):
         step(*args)
 

time: 62.4 us -> 62.1 us (level)
  no operation moved by 1% of the time
where the time goes in v6:
time: 62.1 us; the launch traced here: 62 us
  Pallas kernels  62 us (100%)
    pallas_call x1, Pallas kernels, per_device(): pl.pallas_call(kernel, out_shape=jax.ShapeDtypeStruct((2 * SHARD, ROWS),...  60.4 us
    pallas_call x1, Pallas kernels, per_device(): pl.pallas_call(hand_over, out_shape=jax.ShapeDtypeStruct(result.shape, re...  1.57 us

profile of v6, /device:TPU:1, one launch (start us, length us, event | category | flops | bytes accessed | tf_op | source)
XLA Modules:
  0.0 62.0 jit_solution(14382584208826659040)
XLA Ops:
  0.0 60.4 %shard_map.37.sums = bf16[64,1024]{1,0:T(8,128)(2,1)} custom-call(bf16[1024,2048]{1,0:T(8,128)(2,1)} %a_hbm.1, bf16[32,2048]{1,0:T(8,128)(2,1)} %bitcast.2, s32[8,16]{1,0:T(8,128)} %mask.1), custom_call_target="tpu_custom_call" | custom-call | tf_op jit(solution)/shard_map/pallas_call | solution.py:503
  60.4 1.6 %shard_map.38 = bf16[64,1024]{1,0:T(8,128)(2,1)} custom-call(bf16[64,1024]{1,0:T(8,128)(2,1)} %shard_map.37.sums), custom_call_target="tpu_custom_call" | custom-call | tf_op jit(solution)/shard_map/pallas_call | solution.py:534
